TPU v7x, 256 devices: a whole 4x4x8 slice. The times are simulated.
256 devices in a mesh: space: 128 (over z, x, y_hi, core), tm: 2 (over y_lo).
Axes of the slice: x: 4, y: 4 (y_hi: 2, y_lo: 2; y = y_hi * 2 + y_lo), z: 8, core: 2. Of those that a mesh axis runs over, the one named last changes fastest.
Arguments:
- features: bfloat16 [128, 2, 2, 512, 128], P('space', 'tm'), may hold values from -6 to 6
- cotangent: bfloat16 [128, 2, 2, 512, 128], P('space', 'tm'), may hold values from -6 to 6
- w_first: bfloat16 [27, 128, 128], replicated, may hold values from -0.109375 to 0.109375
- w_second: bfloat16 [27, 128, 128], replicated, may hold values from -0.109375 to 0.109375
- occupancy: int32 [128, 2, 2, 512], P('space', 'tm'), may hold values from 0 to 1, as said below
- neighbors: int32 [128, 2, 2, 27], P('space', 'tm'), may hold values from -1 to 9, as said below
- send_space: int32 [128, 2, 2, 2], P('space', 'tm'), may hold values from -1 to 1, as said below
- send_time: int32 [128, 2, 4], P('space', 'tm'), may hold values from -1 to 5, as said below
Outputs:
- grad_features: bfloat16 [128, 2, 2, 512, 128], P('space', 'tm')
- grad_first: float32 [27, 128, 128], replicated
- grad_second: float32 [27, 128, 128], replicated
Inputs may be any that keep to these rules, and one draw needn't show every extreme that they name: `occupancy`: each device has 1 to 2 active blocks, which come first; on some device all 2 are active. Blocks after the active ones have no occupied voxels. `neighbors`: entries index the extended list of 10 slots; -1 where the neighbouring block is inactive or outside the grid, and in every row of an inactive block. The relation is symmetric: a block's neighbour in one direction has it as neighbour in the opposite direction. `send_space`: positions follow the face's cells; -1 where the cell holds no active block. `send_time`: positions follow the face's cells including one block beyond each slab side, and index the own-plus-space list of 6 slots; -1 where the cell holds no active block or lies outside the grid.
All inputs are finite; a program needn't handle non-finite values.
Results may differ from a plain program's by a relative error of at most 0.0029.
Values may be sent and summed in bfloat16 or wider, within the bound.
No kernel may reach another device: no remote copies, remote signals or barrier semaphores. Data moves between devices by JAX's collectives and lax.ppermute only.
A program may use at most 128 MiB of HBM per device.

v0:
```python
import math
import jax
import jax.numpy as jnp
from jax import lax
from jax.sharding import PartitionSpec as P

EDGE = 8
offsets = [
    (first, second, third) for first in (-1, 0, 1) for second in (-1, 0, 1) for third in (-1, 0, 1)
]


def extended(value, sides, width):
    for axis, dim in sides:
        size, length = (lax.axis_size(axis), value.shape[dim])
        up = [(i, (i + 1) % size) for i in range(size - 1)]
        down = [(j, i) for i, j in up]
        last = lax.slice_in_dim(value, length - width, length, axis=dim)
        initial = lax.slice_in_dim(value, 0, width, axis=dim)
        before = lax.ppermute(last, axis, up)
        after = lax.ppermute(initial, axis, down)
        value = jnp.concatenate([before, value, after], axis=dim)
    return value


def partner(value, axis, bit):
    return lax.ppermute(value, axis, [(i, i ^ 1 << bit) for i in range(lax.axis_size(axis))])


def rim_spans(component, block_edge):
    if component < 0:
        return (slice(block_edge - 1, block_edge), slice(0, 1))
    if component == 0:
        return (slice(0, block_edge), slice(1, block_edge + 1))
    return (slice(0, 1), slice(block_edge + 1, block_edge + 2))


def assemble(store, table, block_edge):
    total_rows = store.shape[0]
    padded = jnp.concatenate([store, jnp.zeros((1,) + store.shape[1:], store.dtype)], axis=0)
    safe_rows = jnp.where(table < 0, total_rows, table)
    pieces = {}
    for number, offset in enumerate(offsets):
        source = [rim_spans(component, block_edge)[0] for component in offset]
        pieces[offset] = jnp.take(
            padded[:, source[0], source[1], source[2]], safe_rows[:, number], axis=0
        )
    layers = []
    for first in (-1, 0, 1):
        columns = []
        for second in (-1, 0, 1):
            columns.append(
                jnp.concatenate([pieces[first, second, third] for third in (-1, 0, 1)], axis=3)
            )
        layers.append(jnp.concatenate(columns, axis=2))
    return jnp.concatenate(layers, axis=1)


def window(canvas, offset, block_edge):
    starts = [1 + component for component in offset]
    region = canvas[
        :,
        starts[0] : starts[0] + block_edge,
        starts[1] : starts[1] + block_edge,
        starts[2] : starts[2] + block_edge,
    ]
    return region.reshape(-1, canvas.shape[-1])


def negate(offset):
    return tuple((-component for component in offset))


def dot_transposed(left, weight):
    return lax.dot_general(
        left, weight, (((1,), (1,)), ((), ())), preferred_element_type=jnp.float32
    )


def dot_outer(left, right):
    return lax.dot_general(
        left, right, (((0,), (0,)), ((), ())), preferred_element_type=jnp.float32
    )


def pick_rows(source, row_index, along_axis):
    size_along = source.shape[along_axis]
    zero_shape = list(source.shape)
    zero_shape[along_axis] = 1
    padded = jnp.concatenate([source, jnp.zeros(zero_shape, source.dtype)], axis=along_axis)
    return jnp.take(padded, jnp.where(row_index < 0, size_along, row_index), axis=along_axis)


def local_pass(x_tile, g_tile, mask_rows, w_first, w_second, block_edge):
    rows = mask_rows.shape[0]
    channels = w_first.shape[-1]
    pre = jnp.zeros((rows, channels), jnp.float32)
    for number, offset in enumerate(offsets):
        pre = pre + jnp.dot(
            window(x_tile, offset, block_edge), w_first[number], preferred_element_type=jnp.float32
        )
    sigmoid_pre = jax.nn.sigmoid(pre)
    hidden = (pre * sigmoid_pre * mask_rows).astype(jnp.bfloat16)
    grad_hidden = jnp.zeros((rows, channels), jnp.float32)
    second_terms = []
    for number, offset in enumerate(offsets):
        back_window = window(g_tile, negate(offset), block_edge)
        grad_hidden = grad_hidden + dot_transposed(back_window, w_second[number])
        second_terms.append(dot_outer(hidden, back_window))
    grad_pre = (grad_hidden * sigmoid_pre * (1.0 + pre * (1.0 - sigmoid_pre)) * mask_rows).astype(
        jnp.bfloat16
    )
    first_terms = [dot_outer(window(x_tile, offset, block_edge), grad_pre) for offset in offsets]
    return (grad_pre, jnp.stack(first_terms), jnp.stack(second_terms))


def body(features, cotangent, w_first, w_second, occupancy, neighbors, send_space, send_time):
    blocks, voxels, channels = (features.shape[2], features.shape[3], features.shape[4])
    block_edge = EDGE
    rim_slots = send_space.shape[3]
    mask_rows = occupancy.reshape(blocks * voxels, 1).astype(jnp.float32)
    mask_cells = occupancy.reshape(blocks, voxels, 1).astype(jnp.bfloat16)
    masked_x = features.reshape(blocks, voxels, channels) * mask_cells
    masked_g = cotangent.reshape(blocks, voxels, channels) * mask_cells
    space_sends = send_space.reshape(2, rim_slots)
    time_sends = send_time.reshape(-1)
    table = neighbors.reshape(blocks, neighbors.shape[3])
    paired = jnp.stack([masked_x, masked_g]).reshape(
        2, blocks, block_edge, block_edge, block_edge, channels
    )
    outgoing = pick_rows(paired, space_sends, 1)
    bordered = extended(outgoing, (("space", 1),), 1)
    below = bordered[:, 0]
    above = bordered[:, 3]
    base = jnp.concatenate([paired, below, above], axis=1)
    toward_time = pick_rows(base, time_sends, 1)
    across = partner(toward_time, "tm", 0)
    shaped = jnp.concatenate([base, across], axis=1)
    x_tile = assemble(shaped[0], table, block_edge)
    g_tile = assemble(shaped[1], table, block_edge)
    grad_pre, first_part, second_part = local_pass(
        x_tile, g_tile, mask_rows, w_first, w_second, block_edge
    )
    da_cells = grad_pre.reshape(blocks, block_edge, block_edge, block_edge, channels)
    da_out = pick_rows(da_cells, space_sends, 0)
    da_border = extended(da_out, (("space", 0),), 1)
    da_below = da_border[0]
    da_above = da_border[3]
    da_base = jnp.concatenate([da_cells, da_below, da_above], axis=0)
    da_toward = pick_rows(da_base, time_sends, 0)
    da_across = partner(da_toward, "tm", 0)
    da_store = jnp.concatenate([da_base, da_across], axis=0)
    da_tile = assemble(da_store, table, block_edge)
    conv_rows = jnp.zeros((blocks * voxels, channels), jnp.float32)
    for number, offset in enumerate(offsets):
        conv_rows = conv_rows + dot_transposed(
            window(da_tile, negate(offset), block_edge), w_first[number]
        )
    grad_rows = (
        cotangent.reshape(blocks * voxels, channels).astype(jnp.float32) + conv_rows * mask_rows
    )
    grad_features = grad_rows.astype(jnp.bfloat16).reshape(features.shape)
    scale = 1.0 / math.sqrt(lax.axis_size("space") * lax.axis_size("tm") * blocks * voxels)
    first_sum, second_sum = lax.psum((first_part, second_part), ("space", "tm"))
    return (grad_features, first_sum * scale, second_sum * scale)


def solution(mesh):
    placed = (
        P("space", "tm", None, None, None),
        P("space", "tm", None, None, None),
        P(),
        P(),
        P("space", "tm", None, None),
        P("space", "tm", None, None),
        P("space", "tm", None, None),
        P("space", "tm", None),
    )
    return jax.shard_map(
        body,
        mesh=mesh,
        in_specs=placed,
        out_specs=(P("space", "tm", None, None, None), P(), P()),
        check_vma=False,
    )
```

profile of v0, /device:TPU:97, one launch (start us, length us, event | category | flops | bytes accessed | tf_op | source)
XLA Modules:
  0.0 582.6 jit_solution(6243704931924489264)
XLA Ops:
  13.6 5.4 collective-permute-start
  19.0 1.9 collective-permute-start.1
  48.8 17.5 %collective-permute-done.2 = bf16[2,4,8,8,8,128]{5,4,3,2,0,1:T(8,128)(2,1)S(1)} collective-permute-done((bf16[2,4,8,8,8,128]{5,4,3,2,0,1:T(8,128)(2,1)S(1)}, bf16[2,4,8,8,8,128]{5,4,3,2,0,1:T(8,128)(2,1)S(1)}, u32[]{:S(2)}, u32[]{:S(2)}) %collective-permute-start.2) | collective-permute-done | bytes 1048608 | tf_op jit(solution)/shard_map/ppermute | solution.py:27
  67.3 2.3 slice_bitcast_fusion
  78.5 1.4 fusion.235
  79.8 1.5 fusion.239
  83.6 2.0 gather_fusion.6
  85.6 2.2 gather_fusion.41
  87.8 2.2 gather_fusion.5
  90.8 1.4 copy.318
  92.1 1.3 gather_fusion.40
  93.4 1.4 gather_fusion.4
  94.8 1.3 bitcast_select_fusion.22
  108.7 1.3 gather_fusion.57
  110.0 2.0 gather_fusion.50
  112.0 2.0 gather_fusion.14
  114.0 1.4 copy.304
  115.4 1.4 copy.314
  116.8 1.4 gather_fusion.52
  118.2 1.4 gather_fusion.16
  119.6 1.4 copy.303
  121.0 1.4 copy.313
  122.4 2.0 gather_fusion.54
  124.4 2.0 gather_fusion.18
  126.4 2.0 gather_fusion.20
  128.4 2.0 gather_fusion.56
  130.4 2.2 gather_fusion.53
  132.6 2.2 gather_fusion.17
  134.8 1.4 copy.305
  136.2 1.4 copy.315
  137.6 2.0 gather_fusion.48
  139.6 2.0 gather_fusion.12
  141.6 1.3 gather_fusion.47
  142.8 2.2 gather_fusion.11
  147.9 1.3 gather_fusion.10
  150.2 1.7 copy.294
  151.9 1.3 gather_fusion.43
  153.2 1.6 gather_fusion.7
  154.8 1.5 bitcast_select_fusion.7
  158.0 1.6 gather_fusion.45
  176.3 1.4 fusion.243
  181.2 1.4 gather_fusion.32
  185.0 1.4 gather_fusion.38
  186.5 1.6 gather_fusion.35
  188.7 1.5 fusion.244
  193.6 1.4 fusion.246
  201.7 1.4 gather_fusion.29
  203.2 1.4 gather_fusion.23
  204.7 1.6 gather_fusion.26
  277.5 7.5 %collective-permute-start.3 = (bf16[1,2,8,8,8,128]{5,4,3,2,1,0:T(8,128)(2,1)S(1)}, bf16[1,2,8,8,8,128]{5,4,3,2,1,0:T(8,128)(2,1)S(1)}, u32[]{:S(2)}, u32[]{:S(2)}) collective-permute-start(bf16[1,2,8,8,8,128]{5,4,3,2,1,0:T(8,128)(2,1)S(1)} %get-tuple-element.195), channel_id=1, source_target_pairs={{0,2},{2,4},{4,6},{6,8},{8,10},{10,12},{12,14},{14,16},{16,18},{18... | collective-permute-start | bytes 786440 | tf_op jit(solution)/shard_map/ppermute | solution.py:20
  285.0 1.9 collective-permute-start.4
  288.7 7.3 %collective-permute-done.4 = bf16[1,2,8,8,8,128]{5,4,3,2,1,0:T(8,128)(2,1)S(1)} collective-permute-done((bf16[1,2,8,8,8,128]{5,4,3,2,1,0:T(8,128)(2,1)S(1)}, bf16[1,2,8,8,8,128]{5,4,3,2,1,0:T(8,128)(2,1)S(1)}, u32[]{:S(2)}, u32[]{:S(2)}) %collective-permute-start.4) | collective-permute-done | bytes 262176 | tf_op jit(solution)/shard_map/ppermute | solution.py:21
  298.5 13.6 %collective-permute-done.5 = bf16[4,8,8,8,128]{4,3,2,1,0:T(8,128)(2,1)} collective-permute-done((bf16[4,8,8,8,128]{4,3,2,1,0:T(8,128)(2,1)}, bf16[4,8,8,8,128]{4,3,2,1,0:T(8,128)(2,1)}, u32[]{:S(2)}, u32[]{:S(2)}) %collective-permute-start.5) | collective-permute-done | bytes 524320 | tf_op jit(solution)/shard_map/ppermute | solution.py:27
  319.2 1.7 gather_fusion.59
  326.2 1.6 gather_fusion.80
  328.5 1.6 gather_fusion.65
  334.7 1.4 gather_fusion.83
  336.2 1.4 gather_fusion.77
  343.0 1.5 fusion.241
  345.6 1.6 gather_fusion.71
  348.9 1.4 gather_fusion.74
  365.0 206.1 %all-reduce.7.cloned.1.call-done = (f32[27,128,128]{2,1,0:T(8,128)}, f32[27,128,128]{2,1,0:T(8,128)}) async-done(((f32[27,128,128]{2,1,0:T(8,128)}, f32[27,128,128]{2,1,0:T(8,128)}), (f32[27,128,128]{2,1,0:T(8,128)}, f32[27,128,128]{2,1,0:T(8,128)})) %all-reduce.7.cloned.1.call-update) | async-done | bytes 3538960 | tf_op jit(solution)/shard_map/psum | solution.py:164
  571.1 3.0 broadcast_multiply_fusion
  574.1 1.4 broadcast_multiply_fusion.1
  (693 shorter events, 212.3 us)
Async XLA Ops:
  7.2 563.9 %all-reduce.7.cloned.1.call-start = ((), (), s32[]{:S(2)}) async-start(), calls=%async_computation | async-start | bytes 7077888 | tf_op jit(solution)/shard_map/psum | solution.py:164
  8.6 4.7 copy-start.120
  13.5 7.4 %copy-start.125 = (s32[1,1,4]{2,1,0:T(1,128)S(1)}, s32[1,1,4]{2,1,0:T(1,128)}, u32[]{:S(2)}) copy-start(s32[1,1,4]{2,1,0:T(1,128)} %param.31) | copy-start | bytes 52
  13.6 28.7 %collective-permute-start = (bf16[2,1,2,8,8,8,128]{6,5,4,3,2,0,1:T(8,128)(2,1)S(1)}, bf16[2,1,2,8,8,8,128]{6,5,4,3,2,0,1:T(8,128)(2,1)S(1)}, u32[]{:S(2)}, u32[]{:S(2)}) collective-permute-start(bf16[2,1,2,8,8,8,128]{6,5,4,3,2,0,1:T(8,128)(2,1)S(1)} %get-tuple-element.121), channel_id=1, source_target_pairs={{0,2},{2,4},{4,6},{6,8},{8,10},{10,12},{12,14},{14,16},{16,18},{18... | collective-permute-start | bytes 1572872 | tf_op jit(solution)/shard_map/ppermute | solution.py:20
  19.0 23.3 %collective-permute-start.1 = (bf16[2,1,2,8,8,8,128]{6,5,4,3,2,0,1:T(8,128)(2,1)S(1)}, bf16[2,1,2,8,8,8,128]{6,5,4,3,2,0,1:T(8,128)(2,1)S(1)}, u32[]{:S(2)}, u32[]{:S(2)}) collective-permute-start(bf16[2,1,2,8,8,8,128]{6,5,4,3,2,0,1:T(8,128)(2,1)S(1)} %get-tuple-element.120), channel_id=1, source_target_pairs={{2,0},{4,2},{6,4},{8,6},{10,8},{12,10},{14,12},{16,14},{18,16},{20... | collective-permute-start | bytes 1572872 | tf_op jit(solution)/shard_map/ppermute | solution.py:21
  20.9 23.3 %copy-start.122 = (pred[4]{0:T(512)(128)(4,1)}, pred[4]{0:T(512)(128)(4,1)S(1)}, u32[]{:S(2)}) copy-start(pred[4]{0:T(512)(128)(4,1)S(1)} %compare_and_fusion.27) | copy-start | bytes 16
  28.0 15.4 %copy-start.104 = (s32[1024]{0:T(1024)}, s32[1024]{0:T(1024)S(1)}, u32[]{:S(2)}) copy-start(s32[1024]{0:T(1024)S(1)} %pad_clamp_fusion.27) | copy-start | bytes 12292
  44.2 2.9 copy-start.38
  44.2 3.7 copy-start.40
  44.4 21.8 %collective-permute-start.2 = (bf16[2,4,8,8,8,128]{5,4,3,2,0,1:T(8,128)(2,1)S(1)}, bf16[2,4,8,8,8,128]{5,4,3,2,0,1:T(8,128)(2,1)S(1)}, u32[]{:S(2)}, u32[]{:S(2)}) collective-permute-start(bf16[2,4,8,8,8,128]{5,4,3,2,0,1:T(8,128)(2,1)S(1)} %select_bitcast_fusion), channel_id=1, source_target_pairs={{0,1},{1,0},{2,3},{3,2},{4,5},{5,4},{6,7},{7,6},{8,9},{9,8},{10,11... | collective-permute-start | bytes 3145736 | tf_op jit(solution)/shard_map/ppermute | solution.py:27
  150.2 11.6 %copy-start.86 = (bf16[2,8,128]{2,1,0:T(8,128)(2,1)S(1)}, bf16[2,8,128]{2,1,0:T(8,128)(2,1)}, u32[]{:S(2)}) copy-start(bf16[2,8,128]{2,1,0:T(8,128)(2,1)} %gather_fusion.42) | copy-start | bytes 12292
  150.2 11.6 %copy-start.87 = (bf16[2,8,128]{2,1,0:T(8,128)(2,1)S(1)}, bf16[2,8,128]{2,1,0:T(8,128)(2,1)}, u32[]{:S(2)}) copy-start(bf16[2,8,128]{2,1,0:T(8,128)(2,1)} %gather_fusion.6) | copy-start | bytes 12292
  154.8 14.7 %copy-start.66 = (bf16[2,8,8,128]{3,2,1,0:T(8,128)(2,1)S(1)}, bf16[2,8,8,128]{3,2,1,0:T(8,128)(2,1)}, u32[]{:S(2)}) copy-start(bf16[2,8,8,128]{3,2,1,0:T(8,128)(2,1)} %gather_fusion.53) | copy-start | bytes 98308
  154.8 14.7 %copy-start.67 = (bf16[2,8,8,128]{3,2,1,0:T(8,128)(2,1)S(1)}, bf16[2,8,8,128]{3,2,1,0:T(8,128)(2,1)}, u32[]{:S(2)}) copy-start(bf16[2,8,8,128]{3,2,1,0:T(8,128)(2,1)} %gather_fusion.17) | copy-start | bytes 98308
  156.2 14.7 %copy-start.68 = (bf16[2,8,8,128]{3,2,1,0:T(8,128)(2,1)S(1)}, bf16[2,8,8,128]{3,2,1,0:T(8,128)(2,1)}, u32[]{:S(2)}) copy-start(bf16[2,8,8,128]{3,2,1,0:T(8,128)(2,1)} %gather_fusion.47) | copy-start | bytes 98308
  156.3 14.7 %copy-start.69 = (bf16[2,8,8,128]{3,2,1,0:T(8,128)(2,1)S(1)}, bf16[2,8,8,128]{3,2,1,0:T(8,128)(2,1)}, u32[]{:S(2)}) copy-start(bf16[2,8,8,128]{3,2,1,0:T(8,128)(2,1)} %gather_fusion.11) | copy-start | bytes 98308
  177.7 3.4 copy-start.98
  177.8 4.9 copy-start.91
  177.8 5.6 copy-start.100
  177.8 6.4 %copy-start.102 = (pred[2]{0:T(512)(128)(4,1)S(1)}, pred[2]{0:T(512)(128)(4,1)}, u32[]{:S(2)}) copy-start(pred[2]{0:T(512)(128)(4,1)} %get-tuple-element.270) | copy-start | bytes 10
  177.8 7.1 %copy-start.95 = (pred[2]{0:T(512)(128)(4,1)S(1)}, pred[2]{0:T(512)(128)(4,1)}, u32[]{:S(2)}) copy-start(pred[2]{0:T(512)(128)(4,1)} %get-tuple-element.271) | copy-start | bytes 10
  177.8 8.6 %copy-start.93 = (pred[2]{0:T(512)(128)(4,1)S(1)}, pred[2]{0:T(512)(128)(4,1)}, u32[]{:S(2)}) copy-start(pred[2]{0:T(512)(128)(4,1)} %get-tuple-element.269) | copy-start | bytes 10
  177.8 10.3 %copy-start.90 = (pred[2]{0:T(512)(128)(4,1)S(1)}, pred[2]{0:T(512)(128)(4,1)}, u32[]{:S(2)}) copy-start(pred[2]{0:T(512)(128)(4,1)} %get-tuple-element.272) | copy-start | bytes 10
  195.1 2.8 copy-start.79
  195.1 3.6 copy-start.78
  195.1 4.3 copy-start.77
  277.3 10.5 %copy-start.44 = (bf16[2,8,8,8,128]{4,3,2,1,0:T(8,128)(2,1)S(1)}, bf16[2,8,8,8,128]{4,3,2,1,0:T(8,128)(2,1)}, u32[]{:S(2)}) copy-start(bf16[2,8,8,8,128]{4,3,2,1,0:T(8,128)(2,1)} %get-tuple-element.140) | copy-start | bytes 786436
  277.5 11.3 %collective-permute-start.3 = (bf16[1,2,8,8,8,128]{5,4,3,2,1,0:T(8,128)(2,1)S(1)}, bf16[1,2,8,8,8,128]{5,4,3,2,1,0:T(8,128)(2,1)S(1)}, u32[]{:S(2)}, u32[]{:S(2)}) collective-permute-start(bf16[1,2,8,8,8,128]{5,4,3,2,1,0:T(8,128)(2,1)S(1)} %get-tuple-element.195), channel_id=1, source_target_pairs={{0,2},{2,4},{4,6},{6,8},{8,10},{10,12},{12,14},{14,16},{16,18},{18... | collective-permute-start | bytes 786440 | tf_op jit(solution)/shard_map/ppermute | solution.py:20
  285.0 11.1 %collective-permute-start.4 = (bf16[1,2,8,8,8,128]{5,4,3,2,1,0:T(8,128)(2,1)S(1)}, bf16[1,2,8,8,8,128]{5,4,3,2,1,0:T(8,128)(2,1)S(1)}, u32[]{:S(2)}, u32[]{:S(2)}) collective-permute-start(bf16[1,2,8,8,8,128]{5,4,3,2,1,0:T(8,128)(2,1)S(1)} %get-tuple-element.194), channel_id=1, source_target_pairs={{2,0},{4,2},{6,4},{8,6},{10,8},{12,10},{14,12},{16,14},{18,16},{20... | collective-permute-start | bytes 786440 | tf_op jit(solution)/shard_map/ppermute | solution.py:21
  297.9 14.2 %collective-permute-start.5 = (bf16[4,8,8,8,128]{4,3,2,1,0:T(8,128)(2,1)}, bf16[4,8,8,8,128]{4,3,2,1,0:T(8,128)(2,1)}, u32[]{:S(2)}, u32[]{:S(2)}) collective-permute-start(bf16[4,8,8,8,128]{4,3,2,1,0:T(8,128)(2,1)} %broadcast_select_fusion), channel_id=1, source_target_pairs={{0,1},{1,0},{2,3},{3,2},{4,5},{5,4},{6,7},{7,6},{8,9},{9,8},{10,11... | collective-permute-start | bytes 1572872 | tf_op jit(solution)/shard_map/ppermute | solution.py:27
  314.9 6.0 %copy-start.106 = (pred[2]{0:T(512)(128)(4,1)S(1)}, pred[2]{0:T(512)(128)(4,1)}, u32[]{:S(2)}) copy-start(pred[2]{0:T(512)(128)(4,1)} %get-tuple-element.303) | copy-start | bytes 10
  314.9 6.8 %copy-start.112 = (pred[2]{0:T(512)(128)(4,1)S(1)}, pred[2]{0:T(512)(128)(4,1)}, u32[]{:S(2)}) copy-start(pred[2]{0:T(512)(128)(4,1)} %get-tuple-element.302) | copy-start | bytes 10
  314.9 7.6 %copy-start.113 = (pred[2]{0:T(512)(128)(4,1)S(1)}, pred[2]{0:T(512)(128)(4,1)}, u32[]{:S(2)}) copy-start(pred[2]{0:T(512)(128)(4,1)} %get-tuple-element.296) | copy-start | bytes 10
  319.1 11.7 %copy-start.64 = (bf16[11,1,8,1,128]{4,3,2,1,0:T(2,128)(2,1)S(1)}, bf16[11,1,8,1,128]{4,3,2,1,0:T(2,128)(2,1)}, u32[]{:S(2)}) copy-start(bf16[11,1,8,1,128]{4,3,2,1,0:T(2,128)(2,1)} %get-tuple-element.54) | copy-start | bytes 67588
  319.1 13.2 %copy-start.63 = (bf16[11,1,8,1,128]{4,3,2,1,0:T(2,128)(2,1)S(1)}, bf16[11,1,8,1,128]{4,3,2,1,0:T(2,128)(2,1)}, u32[]{:S(2)}) copy-start(bf16[11,1,8,1,128]{4,3,2,1,0:T(2,128)(2,1)} %get-tuple-element.55) | copy-start | bytes 67588
  319.1 13.9 %copy-start.96 = (pred[2]{0:T(512)(128)(4,1)S(1)}, pred[2]{0:T(512)(128)(4,1)}, u32[]{:S(2)}) copy-start(pred[2]{0:T(512)(128)(4,1)} %get-tuple-element.271) | copy-start | bytes 10
  319.1 14.0 %copy-start.62 = (bf16[11,8,1,1,128]{4,3,2,1,0:T(2,128)(2,1)S(1)}, bf16[11,8,1,1,128]{4,3,2,1,0:T(2,128)(2,1)}, u32[]{:S(2)}) copy-start(bf16[11,8,1,1,128]{4,3,2,1,0:T(2,128)(2,1)} %get-tuple-element.61) | copy-start | bytes 67588
  319.1 14.7 %copy-start.124 = (pred[2]{0:T(512)(128)(4,1)S(1)}, pred[2]{0:T(512)(128)(4,1)}, u32[]{:S(2)}) copy-start(pred[2]{0:T(512)(128)(4,1)} %compare_and_fusion.19) | copy-start | bytes 10
  319.2 14.7 %copy-start.61 = (bf16[11,8,1,1,128]{4,3,2,1,0:T(2,128)(2,1)S(1)}, bf16[11,8,1,1,128]{4,3,2,1,0:T(2,128)(2,1)}, u32[]{:S(2)}) copy-start(bf16[11,8,1,1,128]{4,3,2,1,0:T(2,128)(2,1)} %get-tuple-element.62) | copy-start | bytes 67588
  319.2 15.4 %copy-start.111 = (pred[2]{0:T(512)(128)(4,1)S(1)}, pred[2]{0:T(512)(128)(4,1)}, u32[]{:S(2)}) copy-start(pred[2]{0:T(512)(128)(4,1)} %get-tuple-element.298) | copy-start | bytes 10
  320.8 15.3 %copy-start.94 = (pred[2]{0:T(512)(128)(4,1)S(1)}, pred[2]{0:T(512)(128)(4,1)}, u32[]{:S(2)}) copy-start(pred[2]{0:T(512)(128)(4,1)} %get-tuple-element.269) | copy-start | bytes 10
  320.8 16.8 %copy-start.92 = (pred[2]{0:T(512)(128)(4,1)S(1)}, pred[2]{0:T(512)(128)(4,1)}, u32[]{:S(2)}) copy-start(pred[2]{0:T(512)(128)(4,1)} %get-tuple-element.275) | copy-start | bytes 10
  320.9 16.8 %copy-start.76 = (bf16[11,1,1,1,128]{4,3,2,1,0:T(2,128)(2,1)S(1)}, bf16[11,1,1,1,128]{4,3,2,1,0:T(2,128)(2,1)}, u32[]{:S(2)}) copy-start(bf16[11,1,1,1,128]{4,3,2,1,0:T(2,128)(2,1)} %get-tuple-element.43) | copy-start | bytes 8452
  320.9 17.5 %copy-start.101 = (pred[2]{0:T(512)(128)(4,1)S(1)}, pred[2]{0:T(512)(128)(4,1)}, u32[]{:S(2)}) copy-start(pred[2]{0:T(512)(128)(4,1)} %get-tuple-element.268) | copy-start | bytes 10
  321.0 17.5 %copy-start.75 = (bf16[11,1,1,1,128]{4,3,2,1,0:T(2,128)(2,1)S(1)}, bf16[11,1,1,1,128]{4,3,2,1,0:T(2,128)(2,1)}, u32[]{:S(2)}) copy-start(bf16[11,1,1,1,128]{4,3,2,1,0:T(2,128)(2,1)} %get-tuple-element.44) | copy-start | bytes 8452
  321.0 18.2 %copy-start.103 = (pred[2]{0:T(512)(128)(4,1)S(1)}, pred[2]{0:T(512)(128)(4,1)}, u32[]{:S(2)}) copy-start(pred[2]{0:T(512)(128)(4,1)} %get-tuple-element.270) | copy-start | bytes 10
  321.0 18.3 %copy-start.74 = (bf16[11,1,1,1,128]{4,3,2,1,0:T(2,128)(2,1)S(1)}, bf16[11,1,1,1,128]{4,3,2,1,0:T(2,128)(2,1)}, u32[]{:S(2)}) copy-start(bf16[11,1,1,1,128]{4,3,2,1,0:T(2,128)(2,1)} %get-tuple-element.45) | copy-start | bytes 8452
  321.0 19.0 %copy-start.99 = (pred[2]{0:T(512)(128)(4,1)S(1)}, pred[2]{0:T(512)(128)(4,1)}, u32[]{:S(2)}) copy-start(pred[2]{0:T(512)(128)(4,1)} %get-tuple-element.274) | copy-start | bytes 10
  321.0 19.0 %copy-start.73 = (bf16[11,1,1,1,128]{4,3,2,1,0:T(2,128)(2,1)S(1)}, bf16[11,1,1,1,128]{4,3,2,1,0:T(2,128)(2,1)}, u32[]{:S(2)}) copy-start(bf16[11,1,1,1,128]{4,3,2,1,0:T(2,128)(2,1)} %get-tuple-element.42) | copy-start | bytes 8452
  321.0 19.7 %copy-start.119 = (pred[2]{0:T(512)(128)(4,1)S(1)}, pred[2]{0:T(512)(128)(4,1)}, u32[]{:S(2)}) copy-start(pred[2]{0:T(512)(128)(4,1)} %get-tuple-element.276) | copy-start | bytes 10
  344.5 2.7 copy-start.105
  344.5 2.8 copy-start.60
  344.5 3.5 copy-start.110
  344.5 4.3 copy-start.108
  344.5 5.8 copy-start.109
  344.5 6.5 %copy-start.107 = (pred[2]{0:T(512)(128)(4,1)S(1)}, pred[2]{0:T(512)(128)(4,1)}, u32[]{:S(2)}) copy-start(pred[2]{0:T(512)(128)(4,1)} %get-tuple-element.284) | copy-start | bytes 10
  344.5 6.6 %copy-start.72 = (bf16[11,1,1,1,128]{4,3,2,1,0:T(2,128)(2,1)S(1)}, bf16[11,1,1,1,128]{4,3,2,1,0:T(2,128)(2,1)}, u32[]{:S(2)}) copy-start(bf16[11,1,1,1,128]{4,3,2,1,0:T(2,128)(2,1)} %get-tuple-element.47) | copy-start | bytes 8452
  344.5 7.3 %copy-start.117 = (pred[2]{0:T(512)(128)(4,1)S(1)}, pred[2]{0:T(512)(128)(4,1)}, u32[]{:S(2)}) copy-start(pred[2]{0:T(512)(128)(4,1)} %get-tuple-element.279) | copy-start | bytes 10
  344.5 7.4 %copy-start.71 = (bf16[11,1,1,1,128]{4,3,2,1,0:T(2,128)(2,1)S(1)}, bf16[11,1,1,1,128]{4,3,2,1,0:T(2,128)(2,1)}, u32[]{:S(2)}) copy-start(bf16[11,1,1,1,128]{4,3,2,1,0:T(2,128)(2,1)} %get-tuple-element.48) | copy-start | bytes 8452
  344.5 8.0 %copy-start.116 = (pred[2]{0:T(512)(128)(4,1)S(1)}, pred[2]{0:T(512)(128)(4,1)}, u32[]{:S(2)}) copy-start(pred[2]{0:T(512)(128)(4,1)} %get-tuple-element.283) | copy-start | bytes 10
  344.6 8.1 %copy-start.70 = (bf16[11,1,1,1,128]{4,3,2,1,0:T(2,128)(2,1)S(1)}, bf16[11,1,1,1,128]{4,3,2,1,0:T(2,128)(2,1)}, u32[]{:S(2)}) copy-start(bf16[11,1,1,1,128]{4,3,2,1,0:T(2,128)(2,1)} %get-tuple-element.49) | copy-start | bytes 8452
  344.6 8.8 %copy-start.114 = (pred[2]{0:T(512)(128)(4,1)S(1)}, pred[2]{0:T(512)(128)(4,1)}, u32[]{:S(2)}) copy-start(pred[2]{0:T(512)(128)(4,1)} %get-tuple-element.285) | copy-start | bytes 10
  344.6 9.6 %copy-start.115 = (pred[2]{0:T(512)(128)(4,1)S(1)}, pred[2]{0:T(512)(128)(4,1)}, u32[]{:S(2)}) copy-start(pred[2]{0:T(512)(128)(4,1)} %get-tuple-element.277) | copy-start | bytes 10
  571.1 3.0 copy-start.42
  (69 other events, 100.0 us)
Sparse Core Ops, SparseCore 0:
  298.5 272.5 all-reduce.6
where the time goes:
time: 591 us; the launch traced here: 583 us
  waiting for transfers between devices  245 us (41%)
  local copies, waits for them, and re-layouts  168 us (28%)
  matrix products  71.6 us (12%)
  other arithmetic  63.2 us (11%)
  starting transfers between devices  18.1 us (3%)
  between operations  17.1 us (3%)
    psum x1, waiting for transfers between devices, body(): first_sum, second_sum = lax.psum((first_part, second_part), ('space', 'tm'))  206 us
    gather x81, local copies, waits for them, and re-layouts, assemble(): jnp.take(padded[:, source[0], source[1], source[2]], safe_rows[:, number]...  97.2 us
    dot_general x54, matrix products, dot_transposed(): lax.dot_general(left, weight, (((1,), (1,)), ((), ())), preferred_element...  34.2 us
    unnamed x313, local copies, waits for them, and re-layouts  33.7 us
    dot_general x54, matrix products, dot_outer(): lax.dot_general(left, right, (((0,), (0,)), ((), ())), preferred_element_...  31.7 us
    ppermute x2, waiting for transfers between devices, partner(): lax.ppermute(value, axis, [(i, i ^ 1 << bit) for i in range(lax.axis_size...  31.1 us
    select_n x81, other arithmetic, assemble(): jnp.take(padded[:, source[0], source[1], source[2]], safe_rows[:, number]...  22.3 us
    gather x23, other arithmetic  13.7 us
  transfers between devices with their start and end apart: 7, of which 4 were waited for; matrix products, arithmetic and copies ran while one was open for 13% of the time, Pallas kernels for 0%

commit v1 on v0

--- a/solution.py
+++ b/solution.py
@@ -161,7 +161,7 @@
     )
     grad_features = grad_rows.astype(jnp.bfloat16).reshape(features.shape)
     scale = 1.0 / math.sqrt(lax.axis_size("space") * lax.axis_size("tm") * blocks * voxels)
-    first_sum, second_sum = lax.psum((first_part, second_part), ("space", "tm"))
+    first_sum, second_sum = lax.psum(lax.psum((first_part, second_part), "tm"), "space")
     return (grad_features, first_sum * scale, second_sum * scale)
 
 

time: 591 us -> 1690 us (2.86)
  the two profiles are of different devices: /device:TPU:97 before, /device:TPU:1 now
where the time goes in v1:
time: 1690 us
  waiting for transfers between devices  1350 us (80%)
  local copies, waits for them, and re-layouts  169 us (10%)
  matrix products  71.6 us (4%)
  other arithmetic  63.4 us (4%)
  starting transfers between devices  17.7 us (1%)
  between operations  17.2 us (1%)
    psum x1, waiting for transfers between devices, body(): lax.psum(lax.psum((first_part, second_part), 'tm'), 'space')  1260 us
    gather x81, local copies, waits for them, and re-layouts, assemble(): jnp.take(padded[:, source[0], source[1], source[2]], safe_rows[:, number]...  99.4 us
    psum x1, waiting for transfers between devices, body(): lax.psum((first_part, second_part), 'tm')  53.2 us
    dot_general x54, matrix products, dot_transposed(): lax.dot_general(left, weight, (((1,), (1,)), ((), ())), preferred_element...  34.2 us
  transfers between devices with their start and end apart: 8, of which 5 were waited for; matrix products, arithmetic and copies ran while one was open for 5% of the time, Pallas kernels for 0%

profile of v1, /device:TPU:1, one launch (start us, length us, event | category | flops | bytes accessed | tf_op | source)
XLA Modules:
  0.0 1685.7 jit_solution(15585695239779384675)
XLA Ops:
  13.6 6.2 collective-permute-start
  19.8 1.9 collective-permute-start.1
  49.8 19.2 %collective-permute-done.2 = bf16[2,4,8,8,8,128]{5,4,3,2,0,1:T(8,128)(2,1)S(1)} collective-permute-done((bf16[2,4,8,8,8,128]{5,4,3,2,0,1:T(8,128)(2,1)S(1)}, bf16[2,4,8,8,8,128]{5,4,3,2,0,1:T(8,128)(2,1)S(1)}, u32[]{:S(2)}, u32[]{:S(2)}) %collective-permute-start.2) | collective-permute-done | bytes 1048608 | tf_op jit(solution)/shard_map/ppermute | solution.py:27
  70.0 2.3 slice_bitcast_fusion
  81.1 1.4 fusion.235
  82.5 1.5 fusion.239
  86.2 2.0 gather_fusion.6
  88.2 2.2 gather_fusion.41
  90.4 2.2 gather_fusion.5
  93.4 1.4 copy.318
  94.8 1.3 gather_fusion.40
  96.1 1.4 gather_fusion.4
  97.5 1.4 bitcast_select_fusion.22
  112.7 2.0 gather_fusion.50
  114.6 2.0 gather_fusion.14
  116.6 1.4 copy.304
  118.0 1.4 copy.314
  119.4 1.4 gather_fusion.52
  120.8 1.4 gather_fusion.16
  122.3 1.4 copy.303
  123.6 1.4 copy.313
  125.0 2.0 gather_fusion.54
  127.0 2.0 gather_fusion.18
  129.0 2.0 gather_fusion.20
  131.0 2.0 gather_fusion.56
  133.0 2.2 gather_fusion.53
  135.2 2.2 gather_fusion.17
  137.4 1.4 copy.305
  138.8 1.4 copy.315
  140.2 2.0 gather_fusion.48
  142.2 2.0 gather_fusion.12
  144.2 1.3 gather_fusion.47
  145.5 2.2 gather_fusion.11
  150.5 1.3 gather_fusion.10
  152.8 1.7 copy.294
  154.5 1.3 gather_fusion.43
  155.8 1.6 gather_fusion.7
  157.4 1.5 bitcast_select_fusion.7
  160.7 1.6 gather_fusion.45
  178.8 1.4 fusion.243
  183.7 1.4 gather_fusion.32
  187.5 1.4 gather_fusion.38
  189.0 1.6 gather_fusion.35
  191.1 1.6 fusion.244
  196.1 1.4 fusion.246
  204.2 1.4 gather_fusion.29
  205.7 1.4 gather_fusion.23
  207.2 1.6 gather_fusion.26
  279.9 5.8 collective-permute-start.3
  285.7 1.9 collective-permute-start.4
  289.4 5.5 collective-permute-done.4
  297.8 9.2 collective-permute-done.5
  314.1 1.8 gather_fusion.59
  319.6 1.6 gather_fusion.80
  321.9 1.6 gather_fusion.65
  327.9 1.4 gather_fusion.83
  330.0 1.4 gather_fusion.77
  339.5 1.6 gather_fusion.71
  342.8 1.4 gather_fusion.74
  344.3 1.4 gather_fusion.68
  355.8 53.2 %all-reduce.11.cloned.1.call-done = (f32[27,128,128]{2,1,0:T(8,128)}, f32[27,128,128]{2,1,0:T(8,128)}) async-done(((f32[27,128,128]{2,1,0:T(8,128)}, f32[27,128,128]{2,1,0:T(8,128)}), (f32[27,128,128]{2,1,0:T(8,128)}, f32[27,128,128]{2,1,0:T(8,128)})) %all-reduce.11.cloned.1.call-update) | async-done | bytes 3538960 | tf_op jit(solution)/shard_map/psum | solution.py:164
  414.8 1259.4 %all-reduce.9.cloned.1.call-done = (f32[27,128,128]{2,1,0:T(8,128)}, f32[27,128,128]{2,1,0:T(8,128)}) async-done(((f32[27,128,128]{2,1,0:T(8,128)}, f32[27,128,128]{2,1,0:T(8,128)}), (f32[27,128,128]{2,1,0:T(8,128)}, f32[27,128,128]{2,1,0:T(8,128)})) %all-reduce.9.cloned.1.call-update) | async-done | bytes 3538960 | tf_op jit(solution)/shard_map/psum | solution.py:164
  1674.2 3.0 broadcast_multiply_fusion
  1677.2 1.4 broadcast_multiply_fusion.1
  (714 shorter events, 215.4 us)
Async XLA Ops:
  7.2 401.8 %all-reduce.11.cloned.1.call-start = ((), (), s32[]{:S(2)}) async-start(), calls=%async_computation.1 | async-start | bytes 7077888 | tf_op jit(solution)/shard_map/psum | solution.py:164
  8.6 4.7 copy-start.127
  13.5 8.2 copy-start.134
  13.6 29.6 %collective-permute-start = (bf16[2,1,2,8,8,8,128]{6,5,4,3,2,0,1:T(8,128)(2,1)S(1)}, bf16[2,1,2,8,8,8,128]{6,5,4,3,2,0,1:T(8,128)(2,1)S(1)}, u32[]{:S(2)}, u32[]{:S(2)}) collective-permute-start(bf16[2,1,2,8,8,8,128]{6,5,4,3,2,0,1:T(8,128)(2,1)S(1)} %get-tuple-element.123), channel_id=1, source_target_pairs={{0,2},{2,4},{4,6},{6,8},{8,10},{10,12},{12,14},{14,16},{16,18},{18... | collective-permute-start | bytes 1572872 | tf_op jit(solution)/shard_map/ppermute | solution.py:20
  19.8 23.4 %collective-permute-start.1 = (bf16[2,1,2,8,8,8,128]{6,5,4,3,2,0,1:T(8,128)(2,1)S(1)}, bf16[2,1,2,8,8,8,128]{6,5,4,3,2,0,1:T(8,128)(2,1)S(1)}, u32[]{:S(2)}, u32[]{:S(2)}) collective-permute-start(bf16[2,1,2,8,8,8,128]{6,5,4,3,2,0,1:T(8,128)(2,1)S(1)} %get-tuple-element.122), channel_id=1, source_target_pairs={{2,0},{4,2},{6,4},{8,6},{10,8},{12,10},{14,12},{16,14},{18,16},{20... | collective-permute-start | bytes 1572872 | tf_op jit(solution)/shard_map/ppermute | solution.py:21
  21.7 23.4 %copy-start.129 = (pred[4]{0:T(512)(128)(4,1)}, pred[4]{0:T(512)(128)(4,1)S(1)}, u32[]{:S(2)}) copy-start(pred[4]{0:T(512)(128)(4,1)S(1)} %compare_and_fusion.27) | copy-start | bytes 16
  28.8 15.6 copy-start.104
  45.1 3.8 copy-start.40
  45.3 23.6 %collective-permute-start.2 = (bf16[2,4,8,8,8,128]{5,4,3,2,0,1:T(8,128)(2,1)S(1)}, bf16[2,4,8,8,8,128]{5,4,3,2,0,1:T(8,128)(2,1)S(1)}, u32[]{:S(2)}, u32[]{:S(2)}) collective-permute-start(bf16[2,4,8,8,8,128]{5,4,3,2,0,1:T(8,128)(2,1)S(1)} %select_bitcast_fusion), channel_id=1, source_target_pairs={{0,1},{1,0},{2,3},{3,2},{4,5},{5,4},{6,7},{7,6},{8,9},{9,8},{10,11... | collective-permute-start | bytes 3145736 | tf_op jit(solution)/shard_map/ppermute | solution.py:27
  152.8 11.6 copy-start.87
  152.8 11.6 copy-start.88
  157.4 14.5 copy-start.61
  157.4 14.5 copy-start.62
  158.9 14.5 copy-start.63
  159.0 14.4 copy-start.64
  180.2 4.9 copy-start.92
  180.2 5.6 copy-start.100
  180.2 6.4 copy-start.102
  180.3 7.1 copy-start.96
  180.3 8.6 copy-start.94
  180.3 10.3 copy-start.91
  197.5 3.6 copy-start.76
  197.5 4.3 copy-start.75
  279.7 8.8 copy-start.44
  279.9 9.5 collective-permute-start.3
  285.7 9.2 collective-permute-start.4
  296.8 10.3 collective-permute-start.5
  297.6 1376.5 %all-reduce.9.cloned.1.call-start = ((), (), s32[]{:S(2)}) async-start(), calls=%async_computation | async-start | bytes 7077888 | tf_op jit(solution)/shard_map/psum | solution.py:164
  309.8 6.1 copy-start.106
  309.8 7.1 copy-start.116
  309.8 7.9 copy-start.117
  310.5 8.0 copy-start.110
  311.2 8.1 copy-start.108
  311.3 8.3 copy-start.109
  312.8 10.7 copy-start.107
  313.5 13.6 copy-start.131
  314.1 9.5 copy-start.58
  314.1 10.9 copy-start.57
  314.1 12.3 copy-start.56
  314.1 13.0 copy-start.55
  314.1 13.7 copy-start.115
  315.9 13.4 copy-start.95
  316.0 15.5 copy-start.93
  316.0 16.1 copy-start.74
  316.0 16.8 copy-start.101
  316.1 17.4 %copy-start.73 = (bf16[11,1,1,1,128]{4,3,2,1,0:T(2,128)(2,1)S(1)}, bf16[11,1,1,1,128]{4,3,2,1,0:T(2,128)(2,1)}, u32[]{:S(2)}) copy-start(bf16[11,1,1,1,128]{4,3,2,1,0:T(2,128)(2,1)} %get-tuple-element.46) | copy-start | bytes 8452
  316.1 18.1 %copy-start.103 = (pred[2]{0:T(512)(128)(4,1)S(1)}, pred[2]{0:T(512)(128)(4,1)}, u32[]{:S(2)}) copy-start(pred[2]{0:T(512)(128)(4,1)} %get-tuple-element.272) | copy-start | bytes 10
  316.1 18.8 %copy-start.72 = (bf16[11,1,1,1,128]{4,3,2,1,0:T(2,128)(2,1)S(1)}, bf16[11,1,1,1,128]{4,3,2,1,0:T(2,128)(2,1)}, u32[]{:S(2)}) copy-start(bf16[11,1,1,1,128]{4,3,2,1,0:T(2,128)(2,1)} %get-tuple-element.47) | copy-start | bytes 8452
  316.1 20.0 %copy-start.71 = (bf16[11,1,1,1,128]{4,3,2,1,0:T(2,128)(2,1)S(1)}, bf16[11,1,1,1,128]{4,3,2,1,0:T(2,128)(2,1)}, u32[]{:S(2)}) copy-start(bf16[11,1,1,1,128]{4,3,2,1,0:T(2,128)(2,1)} %get-tuple-element.44) | copy-start | bytes 8452
  337.7 3.4 copy-start.105
  337.7 3.5 copy-start.54
  337.7 4.2 copy-start.114
  337.7 4.3 copy-start.53
  337.7 5.0 copy-start.112
  337.7 6.5 copy-start.113
  337.7 8.0 copy-start.111
  337.7 8.0 copy-start.70
  337.7 8.7 copy-start.121
  337.8 8.8 copy-start.69
  337.8 9.5 copy-start.120
  337.8 9.6 copy-start.68
  337.8 10.2 copy-start.118
  337.8 10.3 copy-start.67
  337.8 11.0 copy-start.119
  (79 other events, 119.9 us)
Sparse Core Ops, SparseCore 0:
  297.8 111.1 all-reduce.10
  411.7 1262.4 all-reduce.8
